TPU v7x, 512 devices: a whole 4x8x8 slice. The times are simulated.
512 devices in a mesh: tm: 64 (over z, y), state: 8 (over x, core).
Axes of the slice: x: 4, y: 8, z: 8, core: 2. Of those that a mesh axis runs over, the one named last changes fastest.
Arguments:
- offsets: int32 [5], replicated, may hold values from -3 to 3
- coefficients: float32 [5, 2048], replicated, may hold values from 0.1 to 1
- gain_matrix: bfloat16 [64, 1, 2048, 512], P('tm', None, 'state'), may hold values from -0.0625 to 0.0625
- direct_gain: float32 [64, 1, 512], P('tm'), may hold values from 0.2 to 0.8
- observed_cells: int32 [64, 1, 512], P('tm'), may hold values from 0 to 2047
- observed_values: float32 [64, 1, 512], P('tm'), may hold values from -4 to 4
Outputs:
- transition: float32 [64, 2048, 2048], P('tm', None, 'state')
- offset_term: float32 [64, 2048], P('tm')
All inputs are finite; a program needn't handle non-finite values.
Results may differ from a plain program's by a relative error of at most 0.0036.
Values may be sent and summed in bfloat16 or wider, within the bound.
A program may use at most 64 MiB of HBM per device.

v0:
```python
import jax
import jax.numpy as jnp
from jax import lax
from jax.sharding import PartitionSpec as P


def from_behind(value, axis, steps):
    count = lax.axis_size(axis)
    leading, last = (max(0, -steps), min(count, count - steps))
    return lax.ppermute(value, axis, [(source, source + steps) for source in range(leading, last)])


def advance(matrix, step_gains, cells_used, weights, offsets, forcing):
    spread = weights[0][:, None] * jnp.roll(matrix, -offsets[0], axis=0)
    for tap_index in range(1, weights.shape[0]):
        spread = spread + weights[tap_index][:, None] * jnp.roll(
            matrix, -offsets[tap_index], axis=0
        )
    picked = jnp.take(spread, cells_used[0], axis=0)
    if forcing is not None:
        picked = picked - forcing[0][:, None]
    correction = jnp.dot(
        step_gains[0], picked.astype(jnp.bfloat16), preferred_element_type=jnp.float32
    )
    matrix = spread - correction
    return matrix


def local_gain_rows(gain_matrix, direct_gain, observed_cells):
    row_count = gain_matrix.shape[2]
    first_row = lax.axis_index("state") * row_count
    cell_ids = first_row + lax.broadcasted_iota(jnp.int32, gain_matrix.shape[1:], 1)
    observed_hit = cell_ids == observed_cells[0][:, None, :]
    extra = jnp.where(
        observed_hit, direct_gain[0][:, None, :], jnp.zeros_like(direct_gain[0][:, None, :])
    )
    return (gain_matrix[0].astype(jnp.float32) + extra).astype(jnp.bfloat16)


def shards(offsets, coefficients, gain_matrix, direct_gain, observed_cells, observed_values):
    weights = coefficients / jnp.sum(coefficients, axis=0, keepdims=True)
    gain_rows = local_gain_rows(gain_matrix, direct_gain, observed_cells)
    gain_full = lax.all_gather(gain_rows, "state", axis=1, tiled=True)
    cells_used = observed_cells[0]
    forcing = observed_values[0]
    cell_count = gain_full.shape[1]
    columns = gain_rows.shape[1]
    first_column = lax.axis_index("state") * columns
    row_ids = lax.broadcasted_iota(jnp.int32, (cell_count, columns), 0)
    column_ids = first_column + lax.broadcasted_iota(jnp.int32, (cell_count, columns), 1)
    identity_panel = (row_ids == column_ids).astype(jnp.float32)
    span_index = lax.axis_index("tm")

    def own_map(matrix, forced_values=None):
        return advance(matrix, gain_full, cells_used, weights, offsets, forced_values)

    level_zero_trans = own_map(identity_panel)
    level_zero_shift = own_map(jnp.zeros((cell_count, 1), jnp.float32), forcing)
    left_trans, left_shift = from_behind((level_zero_trans, level_zero_shift), "tm", 1)
    level_one_trans = jnp.where(span_index >= 1, own_map(left_trans), level_zero_trans)
    level_one_shift = jnp.where(
        span_index >= 1, own_map(left_shift) + level_zero_shift, level_zero_shift
    )
    far_trans, far_shift = from_behind((level_one_trans, level_one_shift), "tm", 2)
    far_trans = jnp.where(span_index == 1, identity_panel, far_trans)
    earlier_gains, earlier_cells = from_behind((gain_full, cells_used), "tm", 1)
    carried_trans = own_map(
        advance(far_trans, earlier_gains, earlier_cells, weights, offsets, None)
    )
    carried_shift = own_map(
        advance(far_shift, earlier_gains, earlier_cells, weights, offsets, None)
    )
    first_carried = 1
    transition = jnp.where(span_index >= first_carried, carried_trans, level_one_trans)
    offset_term = jnp.where(span_index >= 2, carried_shift + level_one_shift, level_one_shift)
    return (transition[None], offset_term[:, 0][None])


def solution(mesh):
    in_specs = (
        P(),
        P(),
        P("tm", None, "state", None),
        P("tm", None, None),
        P("tm", None, None),
        P("tm", None, None),
    )
    out_specs = (P("tm", None, "state"), P("tm", None))
    return jax.shard_map(shards, mesh=mesh, in_specs=in_specs, out_specs=out_specs, check_vma=False)
```

profile of v0, /device:TPU:24, one launch (start us, length us, event | category | flops | bytes accessed | tf_op | source)
XLA Modules:
  0.0 283.7 jit_solution(14787118618400152176)
XLA Ops:
  7.2 0.0 all-gather.2.cloned.1.call-start
  7.2 1.8 fusion.67
  9.1 0.0 all-gather.2.cloned.1.call-update
  9.1 4.7 %collective-permute-start.3 = (s32[1,512]{1,0:T(1,128)}, s32[1,512]{1,0:T(1,128)S(1)}, u32[]{:S(2)}, u32[]{:S(2)}) collective-permute-start(s32[1,512]{1,0:T(1,128)} %bitcast.144), channel_id=1, source_target_pairs={{0,8},{8,16},{16,24},{24,32},{32,40},{40,48},{48,56},{56,64},{64,7... | collective-permute-start | bytes 6152 | tf_op jit(solution)/shard_map/ppermute | solution.py:10
  13.8 1.5 fusion.131
  18.6 0.9 reduce_sum.9
  19.5 0.7 compare_select_fusion.1
  20.2 0.9 broadcast_divide_fusion
  21.1 0.2 fusion.66
  21.3 5.6 %fusion.42 = f32[2048,256]{1,0:T(8,128)S(1)} fusion(s32[]{:T(128)S(6)} %select_n.189, f32[2048,256]{1,0:T(8,128)S(1)} %fusion.66, s32[]{:T(128)S(6)} %select_n.181, s32[]{:T(128)S(6)} %select_n.183, s32[]{:T(128)S(6)} %select_n.185, s32[]{:T(128)S(6)} %select_n.187, f32[2048]{0:T(1024)S(1)} %bitcast.127, f32[2048]{0:T(1024)S(1)} %bitcast.131, ...), kind=kLoop, calls=%fused_computation.88 | loop fusion | flops 7340032 | bytes 4235284 | tf_op jit(solution)/shard_map/add | solution.py:16
  27.0 0.0 copy-start.1
  27.0 0.0 copy-start.2
  27.0 1.6 gather_fusion
  28.6 0.4 fusion.89
  28.9 3.1 %gather_fusion.4 = f32[512]{0:T(512)S(1)} fusion(f32[2048]{0:T(1024)S(1)} %bitcast.119, s32[1024]{0:T(1024)S(1)} %pad_clamp_fusion.1), kind=kCustom, calls=%fused_computation.1.clone | custom fusion | bytes 6144 | tf_op jit(solution)/shard_map/jit(_take)/gather | solution.py:19
  32.1 12.9 %all-gather.2.cloned.1.call-done = bf16[1,2048,512]{2,1,0:T(8,128)(2,1)} async-done(((bf16[1,256,512]{2,1,0:T(8,128)(2,1)}), bf16[1,2048,512]{2,1,0:T(8,128)(2,1)}) %all-gather.2.cloned.1.call-update) | async-done | bytes 2097168 | tf_op jit(solution)/shard_map/all_gather | solution.py:43
  45.1 4.5 %convolution_subtract_fusion.3 = f32[2048,256]{1,0:T(8,128)} fusion(f32[2048,256]{1,0:T(8,128)} %copy-done.1, bf16[1,2048,512]{2,1,0:T(8,128)(2,1)} %all-gather.2.cloned.1.call-done, bf16[512,256]{1,0:T(8,128)(2,1)S(1)} %gather_fusion, pred[512]{0:T(512)(128)(4,1)S(1)} %get-tuple-element.9), kind=kOutput, calls=%fused_computation.43 | convolution fusion | flops 537526272 | bytes 6554112 | tf_op jit(solution)/shard_map/dot_general | solution.py:22
  49.6 4.6 %collective-permute-start = (f32[2048,256]{1,0:T(8,128)}, f32[2048,256]{1,0:T(8,128)}, u32[]{:S(2)}, u32[]{:S(2)}) collective-permute-start(f32[2048,256]{1,0:T(8,128)} %convolution_subtract_fusion.3), channel_id=1, source_target_pairs={{0,8},{8,16},{16,24},{24,32},{32,40},{40,48},{48,56},{56,64},{64,7... | collective-permute-start | bytes 6291464 | tf_op jit(solution)/shard_map/ppermute | solution.py:10
  54.2 0.6 fusion.11
  54.8 2.5 collective-permute-start.4
  57.3 0.0 collective-permute-done.3
  57.4 42.5 %collective-permute-done.4 = f32[2048,1]{0,1:T(1,128)S(1)} collective-permute-done((f32[2048,1]{0,1:T(1,128)S(1)}, f32[2048,1]{0,1:T(1,128)S(1)}, u32[]{:S(2)}, u32[]{:S(2)}) %collective-permute-start.4) | collective-permute-done | bytes 8224 | tf_op jit(solution)/shard_map/ppermute | solution.py:10
  99.9 0.2 fusion.92
  100.0 3.1 %gather_fusion.5 = f32[512]{0:T(512)S(1)} fusion(f32[2048]{0:T(1024)S(1)} %bitcast.122, s32[1024]{0:T(1024)S(1)} %pad_clamp_fusion.1), kind=kCustom, calls=%fused_computation.5.clone | custom fusion | bytes 6144 | tf_op jit(solution)/shard_map/jit(_take)/gather | solution.py:19
  103.2 0.6 fusion.10
  103.8 4.4 %collective-permute-start.5 = (f32[2048,1]{0,1:T(1,128)S(1)}, f32[2048,1]{0,1:T(1,128)S(1)}, u32[]{:S(2)}, u32[]{:S(2)}) collective-permute-start(f32[2048,1]{0,1:T(1,128)S(1)} %fusion.10), channel_id=1, source_target_pairs={{0,16},{8,24},{16,32},{24,40},{32,48},{40,56},{48,64},{56,72},{64,... | collective-permute-start | bytes 24584 | tf_op jit(solution)/shard_map/ppermute | solution.py:10
  108.3 3.1 %collective-permute-start.2 = (bf16[1,2048,512]{2,1,0:T(8,128)(2,1)S(1)}, bf16[1,2048,512]{2,1,0:T(8,128)(2,1)}, u32[]{:S(2)}, u32[]{:S(2)}) collective-permute-start(bf16[1,2048,512]{2,1,0:T(8,128)(2,1)S(1)} %copy-done), channel_id=1, source_target_pairs={{0,8},{8,16},{16,24},{24,32},{32,40},{40,48},{48,56},{56,64},{64,7... | collective-permute-start | bytes 6291464 | tf_op jit(solution)/shard_map/ppermute | solution.py:10
  111.4 1.7 constant_dynamic-update-slice_fusion.1
  113.2 1.7 constant_dynamic-update-slice_fusion
  114.9 3.1 %fusion.62 = f32[2048,256]{1,0:T(8,128)} fusion(f32[4096,256]{1,0:T(8,128)S(1)} %constant_dynamic-update-slice_fusion, s32[]{:T(128)S(6)} %select_n.189, s32[]{:T(128)S(6)} %select_n.187, s32[]{:T(128)S(6)} %select_n.185, s32[]{:T(128)S(6)} %select_n.183, s32[]{:T(128)S(6)} %select_n.181, f32[2048]{0:T(1024)S(1)} %bitcast.128, f32[2048]{0:T(1024)S(1)} %bitcast.132, ...), kind=kLoop, calls=%fused_computation.109 | loop fusion | flops 4718592 | bytes 12623892 | tf_op jit(solution)/shard_map/add | solution.py:16
  118.0 3.1 %gather_fusion.1 = bf16[512,256]{1,0:T(8,128)(2,1)S(1)} fusion(f32[2048,256]{1,0:T(8,128)} %fusion.62, s32[1024]{0:T(1024)S(1)} %pad_clamp_fusion.1), kind=kCustom, calls=%fused_computation.2.clone | custom fusion | bytes 526336 | tf_op jit(solution)/shard_map/jit(_take)/gather | solution.py:19
  121.1 3.7 %fusion.1 = f32[2048,256]{1,0:T(8,128)} fusion(f32[2048,256]{1,0:T(8,128)} %convolution_subtract_fusion.3, f32[2048,256]{1,0:T(8,128)} %fusion.62, bf16[1,2048,512]{2,1,0:T(8,128)(2,1)S(1)} %copy-done, pred[]{:T(512)S(6)} %ge.18, bf16[512,256]{1,0:T(8,128)(2,1)S(1)} %gather_fusion.1, pred[512]{0:T(512)(128)(4,1)S(1)} %get-tuple-element.9), kind=kOutput, calls=%fused_computation.42 | convolution fusion | flops 538050560 | bytes 8651265 | tf_op jit(solution)/shard_map/dot_general | solution.py:22
  124.9 5.1 %collective-permute-start.1 = (f32[2048,256]{1,0:T(8,128)}, f32[2048,256]{1,0:T(8,128)}, u32[]{:S(2)}, u32[]{:S(2)}) collective-permute-start(f32[2048,256]{1,0:T(8,128)} %fusion.1), channel_id=1, source_target_pairs={{0,16},{8,24},{16,32},{24,40},{32,48},{40,56},{48,64},{56,72},{64,... | collective-permute-start | bytes 6291464 | tf_op jit(solution)/shard_map/ppermute | solution.py:10
  130.0 0.2 fusion.94
  130.1 3.1 %gather_fusion.6 = f32[512]{0:T(512)S(1)} fusion(f32[2048]{0:T(1024)S(1)} %bitcast.120, s32[1024]{0:T(1024)S(1)} %pad_clamp_fusion), kind=kCustom, calls=%fused_computation.6.clone | custom fusion | bytes 6144 | tf_op jit(solution)/shard_map/jit(_take)/gather | solution.py:19
  133.3 26.4 %collective-permute-done.2 = bf16[1,2048,512]{2,1,0:T(8,128)(2,1)} collective-permute-done((bf16[1,2048,512]{2,1,0:T(8,128)(2,1)S(1)}, bf16[1,2048,512]{2,1,0:T(8,128)(2,1)}, u32[]{:S(2)}, u32[]{:S(2)}) %collective-permute-start.2) | collective-permute-done | bytes 2097184 | tf_op jit(solution)/shard_map/ppermute | solution.py:10
  159.7 2.2 fusion.7
  161.9 0.4 fusion.97
  162.3 3.1 %gather_fusion.7 = f32[512]{0:T(512)S(1)} fusion(f32[2048]{0:T(1024)S(1)} %bitcast.121, s32[1024]{0:T(1024)S(1)} %pad_clamp_fusion.1), kind=kCustom, calls=%fused_computation.7.clone | custom fusion | bytes 6144 | tf_op jit(solution)/shard_map/jit(_take)/gather | solution.py:19
  165.5 1.3 fusion.6
  166.7 82.3 %collective-permute-done.1 = f32[2048,256]{1,0:T(8,128)} collective-permute-done((f32[2048,256]{1,0:T(8,128)}, f32[2048,256]{1,0:T(8,128)}, u32[]{:S(2)}, u32[]{:S(2)}) %collective-permute-start.1) | collective-permute-done | bytes 2097184 | tf_op jit(solution)/shard_map/ppermute | solution.py:10
  249.0 1.9 broadcast_select_fusion
  250.9 6.4 %fusion.28 = f32[2048,256]{1,0:T(8,128)} fusion(s32[]{:T(128)S(6)} %select_n.189, f32[2048,256]{1,0:T(8,128)S(1)} %broadcast_select_fusion, s32[]{:T(128)S(6)} %select_n.181, s32[]{:T(128)S(6)} %select_n.183, s32[]{:T(128)S(6)} %select_n.185, s32[]{:T(128)S(6)} %select_n.187, f32[2048]{0:T(1024)S(1)} %bitcast.129, f32[2048]{0:T(1024)S(1)} %bitcast.133, ...), kind=kLoop, calls=%fused_computation.74 | loop fusion | flops 7340032 | bytes 4235284 | tf_op jit(solution)/shard_map/add | solution.py:16
  257.3 3.1 %gather_fusion.2 = bf16[512,256]{1,0:T(8,128)(2,1)S(1)} fusion(f32[2048,256]{1,0:T(8,128)} %fusion.28, s32[1024]{0:T(1024)S(1)} %pad_clamp_fusion), kind=kCustom, calls=%fused_computation.3.clone | custom fusion | bytes 526336 | tf_op jit(solution)/shard_map/jit(_take)/gather | solution.py:19
  260.5 3.0 %convolution_subtract_fusion.1 = f32[2048,256]{1,0:T(8,128)S(1)} fusion(f32[2048,256]{1,0:T(8,128)} %fusion.28, bf16[1,2048,512]{2,1,0:T(8,128)(2,1)} %collective-permute-done.2, bf16[512,256]{1,0:T(8,128)(2,1)S(1)} %gather_fusion.2, pred[512]{0:T(512)(128)(4,1)S(1)} %get-tuple-element.6), kind=kOutput, calls=%fused_computation.40 | convolution fusion | flops 537526272 | bytes 6554112 | tf_op jit(solution)/shard_map/dot_general | solution.py:22
  263.5 6.4 %fusion.14 = f32[2048,256]{1,0:T(8,128)} fusion(s32[]{:T(128)S(6)} %select_n.189, f32[2048,256]{1,0:T(8,128)S(1)} %convolution_subtract_fusion.1, s32[]{:T(128)S(6)} %select_n.181, s32[]{:T(128)S(6)} %select_n.183, s32[]{:T(128)S(6)} %select_n.185, s32[]{:T(128)S(6)} %select_n.187, f32[2048]{0:T(1024)S(1)} %bitcast.130, f32[2048]{0:T(1024)S(1)} %bitcast.134, ...), kind=kLoop, calls=%fused_computation.60 | loop fusion | flops 7340032 | bytes 4235284 | tf_op jit(solution)/shard_map/add | solution.py:16
  270.0 3.1 %gather_fusion.3 = bf16[512,256]{1,0:T(8,128)(2,1)S(1)} fusion(f32[2048,256]{1,0:T(8,128)} %fusion.14, s32[1024]{0:T(1024)S(1)} %pad_clamp_fusion.1), kind=kCustom, calls=%fused_computation.4.clone | custom fusion | bytes 526336 | tf_op jit(solution)/shard_map/jit(_take)/gather | solution.py:19
  273.1 3.7 %fusion.2 = f32[1,2048,256]{2,1,0:T(8,128)} fusion(f32[2048,256]{1,0:T(8,128)} %fusion.1, f32[2048,256]{1,0:T(8,128)} %fusion.14, bf16[1,2048,512]{2,1,0:T(8,128)(2,1)S(1)} %copy-done, pred[]{:T(512)S(6)} %ge.18, bf16[512,256]{1,0:T(8,128)(2,1)S(1)} %gather_fusion.3, pred[512]{0:T(512)(128)(4,1)S(1)} %get-tuple-element.9), kind=kOutput, calls=%fused_computation.44 | convolution fusion | flops 538050560 | bytes 8651265 | tf_op jit(solution)/shard_map/dot_general | solution.py:22
  (22 shorter events, 0.1 us)
Async XLA Ops:
  7.2 37.9 %all-gather.2.cloned.1.call-start = ((), (), s32[]{:S(2)}) async-start(), calls=%async_computation | async-start | bytes 2359296 | tf_op jit(solution)/shard_map/all_gather | solution.py:43
  9.1 48.3 %collective-permute-start.3 = (s32[1,512]{1,0:T(1,128)}, s32[1,512]{1,0:T(1,128)S(1)}, u32[]{:S(2)}, u32[]{:S(2)}) collective-permute-start(s32[1,512]{1,0:T(1,128)} %bitcast.144), channel_id=1, source_target_pairs={{0,8},{8,16},{16,24},{24,32},{32,40},{40,48},{48,56},{56,64},{64,7... | collective-permute-start | bytes 6152 | tf_op jit(solution)/shard_map/ppermute | solution.py:10
  27.0 5.1 %copy-start.1 = (f32[2048,256]{1,0:T(8,128)}, f32[2048,256]{1,0:T(8,128)S(1)}, u32[]{:S(2)}) copy-start(f32[2048,256]{1,0:T(8,128)S(1)} %fusion.42) | copy-start | bytes 6291460
  27.0 5.1 %copy-start.2 = (s32[1,1,512]{2,1,0:T(1,128)S(1)}, s32[1,1,512]{2,1,0:T(1,128)}, u32[]{:S(2)}) copy-start(s32[1,1,512]{2,1,0:T(1,128)} %param.18) | copy-start | bytes 6148
  45.0 9.1 %copy-start = (bf16[1,2048,512]{2,1,0:T(8,128)(2,1)S(1)}, bf16[1,2048,512]{2,1,0:T(8,128)(2,1)}, u32[]{:S(2)}) copy-start(bf16[1,2048,512]{2,1,0:T(8,128)(2,1)} %all-gather.2.cloned.1.call-done) | copy-start | bytes 6291460
  45.1 9.1 %copy-start.3 = (f32[1,1,512]{2,1,0:T(1,128)S(1)}, f32[1,1,512]{2,1,0:T(1,128)}, u32[]{:S(2)}) copy-start(f32[1,1,512]{2,1,0:T(1,128)} %param.19) | copy-start | bytes 6148
  49.6 61.9 %collective-permute-start = (f32[2048,256]{1,0:T(8,128)}, f32[2048,256]{1,0:T(8,128)}, u32[]{:S(2)}, u32[]{:S(2)}) collective-permute-start(f32[2048,256]{1,0:T(8,128)} %convolution_subtract_fusion.3), channel_id=1, source_target_pairs={{0,8},{8,16},{16,24},{24,32},{32,40},{40,48},{48,56},{56,64},{64,7... | collective-permute-start | bytes 6291464 | tf_op jit(solution)/shard_map/ppermute | solution.py:10
  54.8 45.0 %collective-permute-start.4 = (f32[2048,1]{0,1:T(1,128)S(1)}, f32[2048,1]{0,1:T(1,128)S(1)}, u32[]{:S(2)}, u32[]{:S(2)}) collective-permute-start(f32[2048,1]{0,1:T(1,128)S(1)} %fusion.11), channel_id=1, source_target_pairs={{0,8},{8,16},{16,24},{24,32},{32,40},{40,48},{48,56},{56,64},{64,7... | collective-permute-start | bytes 24584 | tf_op jit(solution)/shard_map/ppermute | solution.py:10
  103.8 7.6 %collective-permute-start.5 = (f32[2048,1]{0,1:T(1,128)S(1)}, f32[2048,1]{0,1:T(1,128)S(1)}, u32[]{:S(2)}, u32[]{:S(2)}) collective-permute-start(f32[2048,1]{0,1:T(1,128)S(1)} %fusion.10), channel_id=1, source_target_pairs={{0,16},{8,24},{16,32},{24,40},{32,48},{40,56},{48,64},{56,72},{64,... | collective-permute-start | bytes 24584 | tf_op jit(solution)/shard_map/ppermute | solution.py:10
  108.3 51.4 %collective-permute-start.2 = (bf16[1,2048,512]{2,1,0:T(8,128)(2,1)S(1)}, bf16[1,2048,512]{2,1,0:T(8,128)(2,1)}, u32[]{:S(2)}, u32[]{:S(2)}) collective-permute-start(bf16[1,2048,512]{2,1,0:T(8,128)(2,1)S(1)} %copy-done), channel_id=1, source_target_pairs={{0,8},{8,16},{16,24},{24,32},{32,40},{40,48},{48,56},{56,64},{64,7... | collective-permute-start | bytes 6291464 | tf_op jit(solution)/shard_map/ppermute | solution.py:10
  124.9 124.1 %collective-permute-start.1 = (f32[2048,256]{1,0:T(8,128)}, f32[2048,256]{1,0:T(8,128)}, u32[]{:S(2)}, u32[]{:S(2)}) collective-permute-start(f32[2048,256]{1,0:T(8,128)} %fusion.1), channel_id=1, source_target_pairs={{0,16},{8,24},{16,32},{24,40},{32,48},{40,56},{48,64},{56,72},{64,... | collective-permute-start | bytes 6291464 | tf_op jit(solution)/shard_map/ppermute | solution.py:10
Sparse Core Ops, SparseCore 0:
  10.1 34.8 all-gather.1
where the time goes:
time: 284 us
  waiting for transfers between devices  164 us (58%)
  other arithmetic  29.1 us (10%)
  local copies, waits for them, and re-layouts  28.6 us (10%)
  starting transfers between devices  24.4 us (9%)
  matrix products  19.8 us (7%)
  between operations  17.7 us (6%)
    ppermute x6, waiting for transfers between devices, from_behind(): lax.ppermute(value, axis, [(source, source + steps) for source in range(l...  151 us
    ppermute x6, starting transfers between devices, from_behind(): lax.ppermute(value, axis, [(source, source + steps) for source in range(l...  24.4 us
    gather x8, local copies, waits for them, and re-layouts, advance(): picked = jnp.take(spread, cells_used[0], axis=0)  23.6 us
    add x8, other arithmetic, advance(): spread + weights[tap_index][:, None] * jnp.roll(matrix, -offsets[tap_inde...  22.7 us
    dot_general x8, matrix products, advance(): jnp.dot(step_gains[0], picked.astype(jnp.bfloat16), preferred_element_typ...  19.8 us
    all_gather x1, waiting for transfers between devices, shards(): gain_full = lax.all_gather(gain_rows, 'state', axis=1, tiled=True)  12.9 us
  transfers between devices with their start and end apart: 7, of which 4 were waited for; matrix products, arithmetic and copies ran while one was open for 17% of the time, Pallas kernels for 0%

commit v1 on v0

--- a/solution.py
+++ b/solution.py
@@ -2,6 +2,7 @@
 import jax.numpy as jnp
 from jax import lax
 from jax.sharding import PartitionSpec as P
+from jax.lax import all_to_all, psum
 
 
 def from_behind(value, axis, steps):
@@ -40,7 +41,15 @@
 def shards(offsets, coefficients, gain_matrix, direct_gain, observed_cells, observed_values):
     weights = coefficients / jnp.sum(coefficients, axis=0, keepdims=True)
     gain_rows = local_gain_rows(gain_matrix, direct_gain, observed_cells)
-    gain_full = lax.all_gather(gain_rows, "state", axis=1, tiled=True)
+    gain_full = jnp.concatenate(
+        all_to_all(
+            jnp.stack([gain_rows for _ in range(psum(1, axis_name="state"))]),
+            axis_name="state",
+            split_axis=0,
+            concat_axis=0,
+        ),
+        axis=1,
+    )
     cells_used = observed_cells[0]
     forcing = observed_values[0]
     cell_count = gain_full.shape[1]

time: 284 us -> 268 us (0.944)
  the two profiles are of different devices: /device:TPU:24 before, /device:TPU:248 now
where the time goes in v1:
time: 268 us; the launch traced here: 267 us
  waiting for transfers between devices  153 us (57%)
  starting transfers between devices  33.3 us (12%)
  local copies, waits for them, and re-layouts  30.8 us (11%)
  other arithmetic  26.8 us (10%)
  matrix products  19 us (7%)
  between operations  4.17 us (2%)
    ppermute x6, waiting for transfers between devices, from_behind(): lax.ppermute(value, axis, [(source, source + steps) for source in range(l...  148 us
    ppermute x6, starting transfers between devices, from_behind(): lax.ppermute(value, axis, [(source, source + steps) for source in range(l...  28.9 us
    gather x8, local copies, waits for them, and re-layouts, advance(): picked = jnp.take(spread, cells_used[0], axis=0)  25.2 us
    add x8, other arithmetic, advance(): spread + weights[tap_index][:, None] * jnp.roll(matrix, -offsets[tap_inde...  23.5 us
    dot_general x8, matrix products, advance(): jnp.dot(step_gains[0], picked.astype(jnp.bfloat16), preferred_element_typ...  19 us
  transfers between devices with their start and end apart: 7, of which 4 were waited for; matrix products, arithmetic and copies ran while one was open for 17% of the time, Pallas kernels for 0%

profile of v1, /device:TPU:248, one launch (start us, length us, event | category | flops | bytes accessed | tf_op | source)
XLA Modules:
  0.0 266.8 jit_solution(9194665640963868079)
XLA Ops:
  0.6 1.1 fusion.61
  1.8 1.5 stack.5
  3.3 4.4 %all-to-all-start = ((bf16[8,1,256,512]{3,2,1,0:T(8,128)(2,1)}), bf16[8,1,256,512]{3,2,1,0:T(8,128)(2,1)S(1)}, u32[]{:S(2)}, u32[]{:S(2)}) async-start(bf16[8,1,256,512]{3,2,1,0:T(8,128)(2,1)} %stack.5), calls=%async_computation | async-start | bytes 4194304 | tf_op jit(solution)/shard_map/all_to_all | solution.py:45
  7.7 0.0 copy-done.1
  7.7 4.7 %collective-permute-start.3 = (s32[1,512]{1,0:T(1,128)S(1)}, s32[1,512]{1,0:T(1,128)S(1)}, u32[]{:S(2)}, u32[]{:S(2)}) collective-permute-start(s32[1,512]{1,0:T(1,128)S(1)} %bitcast.145), channel_id=1, source_target_pairs={{0,8},{8,16},{16,24},{24,32},{32,40},{40,48},{48,56},{56,64},{64,7... | collective-permute-start | bytes 6152 | tf_op jit(solution)/shard_map/ppermute | solution.py:11
  12.4 0.0 copy-done
  12.5 0.0 copy-done.2
  12.5 0.6 fusion.125
  16.4 0.2 fusion.60
  16.6 6.4 %fusion.42 = f32[2048,256]{1,0:T(8,128)} fusion(s32[]{:T(128)S(6)} %select_n.190, f32[2048,256]{1,0:T(8,128)S(1)} %fusion.60, s32[]{:T(128)S(6)} %select_n.182, s32[]{:T(128)S(6)} %select_n.184, s32[]{:T(128)S(6)} %select_n.186, s32[]{:T(128)S(6)} %select_n.188, f32[2048]{0:T(1024)S(1)} %bitcast.128, f32[2048]{0:T(1024)S(1)} %bitcast.132, ...), kind=kLoop, calls=%fused_computation.88 | loop fusion | flops 7340032 | bytes 4235284 | tf_op jit(solution)/shard_map/add | solution.py:17
  23.0 3.1 %gather_fusion = bf16[512,256]{1,0:T(8,128)(2,1)S(1)} fusion(f32[2048,256]{1,0:T(8,128)} %fusion.42, s32[1024]{0:T(1024)S(1)} %pad_clamp_fusion.1), kind=kCustom, calls=%fused_computation.clone | custom fusion | bytes 526336 | tf_op jit(solution)/shard_map/jit(_take)/gather | solution.py:20
  26.2 0.4 fusion.83
  26.6 3.1 %gather_fusion.4 = f32[512]{0:T(512)S(1)} fusion(f32[2048]{0:T(1024)S(1)} %bitcast.113, s32[1024]{0:T(1024)S(1)} %pad_clamp_fusion.1), kind=kCustom, calls=%fused_computation.1.clone | custom fusion | bytes 6144 | tf_op jit(solution)/shard_map/jit(_take)/gather | solution.py:20
  29.7 5.2 %all-to-all-done = bf16[8,1,256,512]{3,2,1,0:T(8,128)(2,1)S(1)} async-done(((bf16[8,1,256,512]{3,2,1,0:T(8,128)(2,1)}), bf16[8,1,256,512]{3,2,1,0:T(8,128)(2,1)S(1)}, u32[]{:S(2)}, u32[]{:S(2)}) %all-to-all-start) | async-done | bytes 2097184 | tf_op jit(solution)/shard_map/all_to_all | solution.py:45
  34.9 3.7 %convolution_subtract_fusion.3 = f32[2048,256]{1,0:T(8,128)} fusion(f32[2048,256]{1,0:T(8,128)} %fusion.42, bf16[2048,512]{1,0:T(8,128)(2,1)S(1)} %bitcast.117, bf16[512,256]{1,0:T(8,128)(2,1)S(1)} %gather_fusion, pred[512]{0:T(512)(128)(4,1)S(1)} %get-tuple-element.9), kind=kOutput, calls=%fused_computation.43 | convolution fusion | flops 537526272 | bytes 6554112 | tf_op jit(solution)/shard_map/dot_general | solution.py:23
  38.7 4.7 %collective-permute-start = (f32[2048,256]{1,0:T(8,128)}, f32[2048,256]{1,0:T(8,128)}, u32[]{:S(2)}, u32[]{:S(2)}) collective-permute-start(f32[2048,256]{1,0:T(8,128)} %convolution_subtract_fusion.3), channel_id=1, source_target_pairs={{0,8},{8,16},{16,24},{24,32},{32,40},{40,48},{48,56},{56,64},{64,7... | collective-permute-start | bytes 6291464 | tf_op jit(solution)/shard_map/ppermute | solution.py:11
  43.4 0.6 fusion.11
  44.0 3.5 %collective-permute-start.4 = (f32[2048,1]{0,1:T(1,128)S(1)}, f32[2048,1]{0,1:T(1,128)S(1)}, u32[]{:S(2)}, u32[]{:S(2)}) collective-permute-start(f32[2048,1]{0,1:T(1,128)S(1)} %fusion.11), channel_id=1, source_target_pairs={{0,8},{8,16},{16,24},{24,32},{32,40},{40,48},{48,56},{56,64},{64,7... | collective-permute-start | bytes 24584 | tf_op jit(solution)/shard_map/ppermute | solution.py:11
  47.5 0.0 collective-permute-done.3
  47.5 40.9 %collective-permute-done.4 = f32[2048,1]{0,1:T(1,128)S(1)} collective-permute-done((f32[2048,1]{0,1:T(1,128)S(1)}, f32[2048,1]{0,1:T(1,128)S(1)}, u32[]{:S(2)}, u32[]{:S(2)}) %collective-permute-start.4) | collective-permute-done | bytes 8224 | tf_op jit(solution)/shard_map/ppermute | solution.py:11
  88.4 0.2 fusion.86
  88.6 3.1 %gather_fusion.5 = f32[512]{0:T(512)S(1)} fusion(f32[2048]{0:T(1024)S(1)} %bitcast.116, s32[1024]{0:T(1024)S(1)} %pad_clamp_fusion.1), kind=kCustom, calls=%fused_computation.5.clone | custom fusion | bytes 6144 | tf_op jit(solution)/shard_map/jit(_take)/gather | solution.py:20
  91.8 0.6 fusion.10
  92.4 5.4 %collective-permute-start.5 = (f32[2048,1]{0,1:T(1,128)S(1)}, f32[2048,1]{0,1:T(1,128)S(1)}, u32[]{:S(2)}, u32[]{:S(2)}) collective-permute-start(f32[2048,1]{0,1:T(1,128)S(1)} %fusion.10), channel_id=1, source_target_pairs={{0,16},{8,24},{16,32},{24,40},{32,48},{40,56},{48,64},{56,72},{64,... | collective-permute-start | bytes 24584 | tf_op jit(solution)/shard_map/ppermute | solution.py:11
  97.8 4.2 %collective-permute-start.2 = (bf16[1,2048,512]{2,1,0:T(8,128)(2,1)S(1)}, bf16[1,2048,512]{2,1,0:T(8,128)(2,1)}, u32[]{:S(2)}, u32[]{:S(2)}) collective-permute-start(bf16[1,2048,512]{2,1,0:T(8,128)(2,1)S(1)} %bitcast.120), channel_id=1, source_target_pairs={{0,8},{8,16},{16,24},{24,32},{32,40},{40,48},{48,56},{56,64},{64,7... | collective-permute-start | bytes 6291464 | tf_op jit(solution)/shard_map/ppermute | solution.py:11
  102.1 0.0 collective-permute-done.5
  102.1 0.0 collective-permute-done
  102.1 1.7 constant_dynamic-update-slice_fusion.1
  103.8 1.7 constant_dynamic-update-slice_fusion
  105.6 3.1 %fusion.56 = f32[2048,256]{1,0:T(8,128)} fusion(f32[4096,256]{1,0:T(8,128)S(1)} %constant_dynamic-update-slice_fusion, s32[]{:T(128)S(6)} %select_n.190, s32[]{:T(128)S(6)} %select_n.188, s32[]{:T(128)S(6)} %select_n.186, s32[]{:T(128)S(6)} %select_n.184, s32[]{:T(128)S(6)} %select_n.182, f32[2048]{0:T(1024)S(1)} %bitcast.129, f32[2048]{0:T(1024)S(1)} %bitcast.133, ...), kind=kLoop, calls=%fused_computation.103 | loop fusion | flops 4718592 | bytes 12623892 | tf_op jit(solution)/shard_map/add | solution.py:17
  108.7 3.1 %gather_fusion.1 = bf16[512,256]{1,0:T(8,128)(2,1)S(1)} fusion(f32[2048,256]{1,0:T(8,128)} %fusion.56, s32[1024]{0:T(1024)S(1)} %pad_clamp_fusion.1), kind=kCustom, calls=%fused_computation.2.clone | custom fusion | bytes 526336 | tf_op jit(solution)/shard_map/jit(_take)/gather | solution.py:20
  111.8 3.7 %fusion.1 = f32[2048,256]{1,0:T(8,128)} fusion(f32[2048,256]{1,0:T(8,128)} %convolution_subtract_fusion.3, f32[2048,256]{1,0:T(8,128)} %fusion.56, bf16[2048,512]{1,0:T(8,128)(2,1)S(1)} %bitcast.121, pred[]{:T(512)S(6)} %ge.18, bf16[512,256]{1,0:T(8,128)(2,1)S(1)} %gather_fusion.1, pred[512]{0:T(512)(128)(4,1)S(1)} %get-tuple-element.9), kind=kOutput, calls=%fused_computation.42 | convolution fusion | flops 538050560 | bytes 8651265 | tf_op jit(solution)/shard_map/dot_general | solution.py:23
  115.6 6.3 %collective-permute-start.1 = (f32[2048,256]{1,0:T(8,128)}, f32[2048,256]{1,0:T(8,128)}, u32[]{:S(2)}, u32[]{:S(2)}) collective-permute-start(f32[2048,256]{1,0:T(8,128)} %fusion.1), channel_id=1, source_target_pairs={{0,16},{8,24},{16,32},{24,40},{32,48},{40,56},{48,64},{56,72},{64,... | collective-permute-start | bytes 6291464 | tf_op jit(solution)/shard_map/ppermute | solution.py:11
  121.9 0.2 fusion.88
  122.1 3.1 %gather_fusion.6 = f32[512]{0:T(512)S(1)} fusion(f32[2048]{0:T(1024)S(1)} %bitcast.114, s32[1024]{0:T(1024)S(1)} %pad_clamp_fusion), kind=kCustom, calls=%fused_computation.6.clone | custom fusion | bytes 6144 | tf_op jit(solution)/shard_map/jit(_take)/gather | solution.py:20
  125.3 67.1 %collective-permute-done.2 = bf16[1,2048,512]{2,1,0:T(8,128)(2,1)} collective-permute-done((bf16[1,2048,512]{2,1,0:T(8,128)(2,1)S(1)}, bf16[1,2048,512]{2,1,0:T(8,128)(2,1)}, u32[]{:S(2)}, u32[]{:S(2)}) %collective-permute-start.2) | collective-permute-done | bytes 2097184 | tf_op jit(solution)/shard_map/ppermute | solution.py:11
  192.3 2.2 fusion.7
  194.6 0.4 fusion.91
  195.0 3.1 %gather_fusion.7 = f32[512]{0:T(512)S(1)} fusion(f32[2048]{0:T(1024)S(1)} %bitcast.115, s32[1024]{0:T(1024)S(1)} %pad_clamp_fusion.1), kind=kCustom, calls=%fused_computation.7.clone | custom fusion | bytes 6144 | tf_op jit(solution)/shard_map/jit(_take)/gather | solution.py:20
  198.1 1.3 fusion.6
  199.4 39.6 %collective-permute-done.1 = f32[2048,256]{1,0:T(8,128)} collective-permute-done((f32[2048,256]{1,0:T(8,128)}, f32[2048,256]{1,0:T(8,128)}, u32[]{:S(2)}, u32[]{:S(2)}) %collective-permute-start.1) | collective-permute-done | bytes 2097184 | tf_op jit(solution)/shard_map/ppermute | solution.py:11
  239.0 1.9 broadcast_select_fusion
  240.9 6.4 %fusion.28 = f32[2048,256]{1,0:T(8,128)} fusion(s32[]{:T(128)S(6)} %select_n.190, f32[2048,256]{1,0:T(8,128)S(1)} %broadcast_select_fusion, s32[]{:T(128)S(6)} %select_n.182, s32[]{:T(128)S(6)} %select_n.184, s32[]{:T(128)S(6)} %select_n.186, s32[]{:T(128)S(6)} %select_n.188, f32[2048]{0:T(1024)S(1)} %bitcast.130, f32[2048]{0:T(1024)S(1)} %bitcast.134, ...), kind=kLoop, calls=%fused_computation.74 | loop fusion | flops 7340032 | bytes 4235284 | tf_op jit(solution)/shard_map/add | solution.py:17
  247.3 3.1 %gather_fusion.2 = bf16[512,256]{1,0:T(8,128)(2,1)S(1)} fusion(f32[2048,256]{1,0:T(8,128)} %fusion.28, s32[1024]{0:T(1024)S(1)} %pad_clamp_fusion), kind=kCustom, calls=%fused_computation.3.clone | custom fusion | bytes 526336 | tf_op jit(solution)/shard_map/jit(_take)/gather | solution.py:20
  250.4 3.0 %convolution_subtract_fusion.1 = f32[2048,256]{1,0:T(8,128)S(1)} fusion(f32[2048,256]{1,0:T(8,128)} %fusion.28, bf16[1,2048,512]{2,1,0:T(8,128)(2,1)} %collective-permute-done.2, bf16[512,256]{1,0:T(8,128)(2,1)S(1)} %gather_fusion.2, pred[512]{0:T(512)(128)(4,1)S(1)} %get-tuple-element.6), kind=kOutput, calls=%fused_computation.40 | convolution fusion | flops 537526272 | bytes 6554112 | tf_op jit(solution)/shard_map/dot_general | solution.py:23
  253.5 6.4 %fusion.14 = f32[2048,256]{1,0:T(8,128)} fusion(s32[]{:T(128)S(6)} %select_n.190, f32[2048,256]{1,0:T(8,128)S(1)} %convolution_subtract_fusion.1, s32[]{:T(128)S(6)} %select_n.182, s32[]{:T(128)S(6)} %select_n.184, s32[]{:T(128)S(6)} %select_n.186, s32[]{:T(128)S(6)} %select_n.188, f32[2048]{0:T(1024)S(1)} %bitcast.131, f32[2048]{0:T(1024)S(1)} %bitcast.135, ...), kind=kLoop, calls=%fused_computation.60 | loop fusion | flops 7340032 | bytes 4235284 | tf_op jit(solution)/shard_map/add | solution.py:17
  259.9 3.1 %gather_fusion.3 = bf16[512,256]{1,0:T(8,128)(2,1)S(1)} fusion(f32[2048,256]{1,0:T(8,128)} %fusion.14, s32[1024]{0:T(1024)S(1)} %pad_clamp_fusion.1), kind=kCustom, calls=%fused_computation.4.clone | custom fusion | bytes 526336 | tf_op jit(solution)/shard_map/jit(_take)/gather | solution.py:20
  263.1 3.7 %fusion.2 = f32[1,2048,256]{2,1,0:T(8,128)} fusion(f32[2048,256]{1,0:T(8,128)} %fusion.1, f32[2048,256]{1,0:T(8,128)} %fusion.14, bf16[2048,512]{1,0:T(8,128)(2,1)S(1)} %bitcast.123, pred[]{:T(512)S(6)} %ge.18, bf16[512,256]{1,0:T(8,128)(2,1)S(1)} %gather_fusion.3, pred[512]{0:T(512)(128)(4,1)S(1)} %get-tuple-element.9), kind=kOutput, calls=%fused_computation.44 | convolution fusion | flops 538050560 | bytes 8651265 | tf_op jit(solution)/shard_map/dot_general | solution.py:23
  (22 shorter events, 0.2 us)
Async XLA Ops:
  3.3 4.4 %copy-start.1 = (s32[1,1,512]{2,1,0:T(1,128)S(1)}, s32[1,1,512]{2,1,0:T(1,128)}, u32[]{:S(2)}) copy-start(s32[1,1,512]{2,1,0:T(1,128)} %param.18) | copy-start | bytes 6148
  3.3 9.2 %copy-start = (f32[5,2048]{1,0:T(8,128)S(1)}, f32[5,2048]{1,0:T(8,128)}, u32[]{:S(2)}) copy-start(f32[5,2048]{1,0:T(8,128)} %param.15) | copy-start | bytes 122884
  3.3 9.3 %copy-start.2 = (s32[5]{0:T(128)S(1)}, s32[5]{0:T(128)}, u32[]{:S(2)}) copy-start(s32[5]{0:T(128)} %param.14) | copy-start | bytes 64
  3.3 31.6 %all-to-all-start = ((bf16[8,1,256,512]{3,2,1,0:T(8,128)(2,1)}), bf16[8,1,256,512]{3,2,1,0:T(8,128)(2,1)S(1)}, u32[]{:S(2)}, u32[]{:S(2)}) async-start(bf16[8,1,256,512]{3,2,1,0:T(8,128)(2,1)} %stack.5), calls=%async_computation | async-start | bytes 4194304 | tf_op jit(solution)/shard_map/all_to_all | solution.py:45
  7.7 39.8 %collective-permute-start.3 = (s32[1,512]{1,0:T(1,128)S(1)}, s32[1,512]{1,0:T(1,128)S(1)}, u32[]{:S(2)}, u32[]{:S(2)}) collective-permute-start(s32[1,512]{1,0:T(1,128)S(1)} %bitcast.145), channel_id=1, source_target_pairs={{0,8},{8,16},{16,24},{24,32},{32,40},{40,48},{48,56},{56,64},{64,7... | collective-permute-start | bytes 6152 | tf_op jit(solution)/shard_map/ppermute | solution.py:11
  34.9 8.4 %copy-start.3 = (f32[1,1,512]{2,1,0:T(1,128)S(1)}, f32[1,1,512]{2,1,0:T(1,128)}, u32[]{:S(2)}) copy-start(f32[1,1,512]{2,1,0:T(1,128)} %param.19) | copy-start | bytes 6148
  38.7 63.4 %collective-permute-start = (f32[2048,256]{1,0:T(8,128)}, f32[2048,256]{1,0:T(8,128)}, u32[]{:S(2)}, u32[]{:S(2)}) collective-permute-start(f32[2048,256]{1,0:T(8,128)} %convolution_subtract_fusion.3), channel_id=1, source_target_pairs={{0,8},{8,16},{16,24},{24,32},{32,40},{40,48},{48,56},{56,64},{64,7... | collective-permute-start | bytes 6291464 | tf_op jit(solution)/shard_map/ppermute | solution.py:11
  44.0 44.4 %collective-permute-start.4 = (f32[2048,1]{0,1:T(1,128)S(1)}, f32[2048,1]{0,1:T(1,128)S(1)}, u32[]{:S(2)}, u32[]{:S(2)}) collective-permute-start(f32[2048,1]{0,1:T(1,128)S(1)} %fusion.11), channel_id=1, source_target_pairs={{0,8},{8,16},{16,24},{24,32},{32,40},{40,48},{48,56},{56,64},{64,7... | collective-permute-start | bytes 24584 | tf_op jit(solution)/shard_map/ppermute | solution.py:11
  92.4 9.7 %collective-permute-start.5 = (f32[2048,1]{0,1:T(1,128)S(1)}, f32[2048,1]{0,1:T(1,128)S(1)}, u32[]{:S(2)}, u32[]{:S(2)}) collective-permute-start(f32[2048,1]{0,1:T(1,128)S(1)} %fusion.10), channel_id=1, source_target_pairs={{0,16},{8,24},{16,32},{24,40},{32,48},{40,56},{48,64},{56,72},{64,... | collective-permute-start | bytes 24584 | tf_op jit(solution)/shard_map/ppermute | solution.py:11
  97.8 94.5 %collective-permute-start.2 = (bf16[1,2048,512]{2,1,0:T(8,128)(2,1)S(1)}, bf16[1,2048,512]{2,1,0:T(8,128)(2,1)}, u32[]{:S(2)}, u32[]{:S(2)}) collective-permute-start(bf16[1,2048,512]{2,1,0:T(8,128)(2,1)S(1)} %bitcast.120), channel_id=1, source_target_pairs={{0,8},{8,16},{16,24},{24,32},{32,40},{40,48},{48,56},{56,64},{64,7... | collective-permute-start | bytes 6291464 | tf_op jit(solution)/shard_map/ppermute | solution.py:11
  115.6 123.4 %collective-permute-start.1 = (f32[2048,256]{1,0:T(8,128)}, f32[2048,256]{1,0:T(8,128)}, u32[]{:S(2)}, u32[]{:S(2)}) collective-permute-start(f32[2048,256]{1,0:T(8,128)} %fusion.1), channel_id=1, source_target_pairs={{0,16},{8,24},{16,32},{24,40},{32,48},{40,56},{48,64},{56,72},{64,... | collective-permute-start | bytes 6291464 | tf_op jit(solution)/shard_map/ppermute | solution.py:11
